TPU v7x, 256 devices: a whole 4x4x8 slice. The times are simulated.
256 devices in a mesh: ctr: 16 (over z, core), row: 16 (over y, x).
Axes of the slice: x: 4, y: 4, z: 8, core: 2. Of those that a mesh axis runs over, the one named last changes fastest.
Arguments:
- features: bfloat16 [440, 131072], P(None, ('ctr', 'row'))
- targets: float32 [128, 131072], P(None, ('ctr', 'row')), may hold values from -6 to 6
- predictions: float32 [128, 131072], P(None, ('ctr', 'row')), may hold values from -6 to 6
- coeffs: float32 [128, 131072], P(None, ('ctr', 'row')), may hold values from -1.2 to 1.2
- members: int32 [1024, 128], replicated, may hold values from 0 to 131071, as said below
- order: int32 [2, 16], replicated, may hold values from 0 to 1023, as said below
Outputs:
- new_predictions: float32 [128, 131072], P(None, ('ctr', 'row'))
- new_coeffs: float32 [128, 131072], P(None, ('ctr', 'row'))
Inputs may be any that keep to these rules, and one draw needn't show every extreme that they name: `members`: every frame index appears exactly once, so the blocks partition the frames. `order`: the 16 blocks of one step are distinct.
All inputs are finite; a program needn't handle non-finite values.
Results may differ from a plain program's by a relative error of at most 0.0019.
Values may be sent and summed in bfloat16 or wider, within the bound.
No kernel may reach another device: no remote copies, remote signals or barrier semaphores. Data moves between devices by JAX's collectives and lax.ppermute only.
A program may use at most 128 MiB of HBM per device.

v0:
```python
import math

import jax
import jax.numpy as jnp
from jax import lax
from jax.sharding import Mesh
from jax.sharding import PartitionSpec as P

STEPS = 2
CTR = ("ctr_0", "ctr_1")
CTR_ROW = ("ctr_0", "ctr_1", "row")


ridge = 2.0


def scatter_axes(array, axes, dim):
    for axis in axes:
        array = lax.psum_scatter(array, axis, scatter_dimension=dim, tiled=True)
    return array


def split_up(array, dim, size):
    before, after = (array.shape[:dim], array.shape[dim + 1 :])
    return jnp.moveaxis(array.reshape(*before, size, -1, *after), dim, 0)


def sum_at_owner(array, axis, dim):
    size = lax.axis_size(axis)
    pieces = lax.all_to_all(split_up(array, dim, size), axis, 0, 0, tiled=True)
    return jnp.sum(pieces, axis=0)


def in_order(pieces, dim):
    dims = list(pieces.shape[1:])
    dims[dim] *= pieces.shape[0]
    return jnp.moveaxis(pieces, 0, dim).reshape(dims)


def sent_to_all(array, axis):
    size = lax.axis_size(axis)
    return lax.all_to_all(
        jnp.broadcast_to(array[None], (size, *array.shape)), axis, 0, 0, tiled=True
    )


def gathered_copies(array, axis, dim):
    return in_order(sent_to_all(array, axis), dim)


def from_behind(array, axis, by):
    size = lax.axis_size(axis)
    pairs = [(i, i + by) for i in range(size) if 0 <= i + by < size]
    return lax.ppermute(array, axis, pairs)


def kernel_tile(left, right):
    scale = 0.25 / math.sqrt(left.shape[0])
    inner = lax.dot_general(
        left, right, (((0,), (0,)), ((), ())), preferred_element_type=jnp.float32
    )
    return jnp.exp(scale * inner)


def invert_block(system):
    factor = jnp.linalg.cholesky(system)
    return jax.scipy.linalg.cho_solve((factor, True), jnp.eye(system.shape[-1], dtype=system.dtype))


def apply_inverse(inverse, rhs):
    return jnp.dot(rhs, inverse, precision=lax.Precision.HIGHEST)


def per_device(features, targets, predictions, coeffs, members, order):
    frames = features.shape[1]
    depth = features.shape[0]
    outputs = targets.shape[0]
    block = members.shape[1]
    owners = lax.axis_size(CTR)
    width = owners * block
    mine = lax.axis_index(CTR)
    base = (mine * lax.axis_size("row") + lax.axis_index("row")) * frames
    ident = jnp.eye(block, dtype=jnp.float32)
    for step in range(STEPS):
        ids = members[order[step]].reshape(-1)
        local = ids - base
        valid = (local >= 0) & (local < frames)
        safe = jnp.clip(local, 0, frames - 1)
        keep = valid[None, :]
        picked = jnp.where(keep, jnp.take(features, safe, axis=1), jnp.zeros((), jnp.bfloat16))
        residue = (
            jnp.take(targets, safe, axis=1)
            - jnp.take(predictions, safe, axis=1)
            - ridge * jnp.take(coeffs, safe, axis=1)
        )
        residue = jnp.where(keep, residue, 0.0)
        own_x = scatter_axes(picked, CTR, 1).astype(jnp.float32)
        own_r = sum_at_owner(residue, CTR, 1)
        stacked = jnp.concatenate([own_x, own_r], axis=0)
        shares = sum_at_owner(stacked, "row", 1)
        stacked = gathered_copies(shares, "row", 1)
        centre = stacked[:depth].astype(jnp.bfloat16)
        start = stacked[depth:]
        all_centres = gathered_copies(centre, CTR, 1)
        column = kernel_tile(all_centres, centre)
        inverse = invert_block(
            lax.dynamic_slice_in_dim(column, mine * block, block, 0) + ridge * ident
        )
        column_bf = column.astype(jnp.bfloat16)

        def advance(state):
            correction = jnp.dot(state, column_bf, preferred_element_type=jnp.float32)
            return apply_inverse(inverse, start - correction).astype(jnp.bfloat16)

        def turn(count, carry):
            state, own = carry
            fresh = advance(state)
            active = mine == count
            own = jnp.where(active, fresh, own)
            placed = lax.dynamic_update_slice(
                state, fresh, (jnp.int32(0), (count * block).astype(jnp.int32))
            )
            state = jnp.where(active, placed, state)
            state = from_behind(state, CTR, 1)
            return (state, own)

        empty = jnp.zeros((outputs, width), jnp.bfloat16)
        state, own = lax.fori_loop(
            0, owners - 1, turn, (empty, jnp.zeros((outputs, block), jnp.bfloat16))
        )
        own = jnp.where(mine == owners - 1, advance(state), own)
        deltas = gathered_copies(own, CTR, 1)
        tile = kernel_tile(all_centres, features).astype(jnp.bfloat16)
        predictions = predictions + jnp.dot(deltas, tile, preferred_element_type=jnp.float32)
        coeffs = coeffs.at[:, safe].add(jnp.where(keep, deltas.astype(jnp.float32), 0.0))
    return (predictions, coeffs)


def solution(mesh):
    torus = Mesh(mesh.devices.reshape(8, 2, mesh.shape["row"]), ("ctr_0", "ctr_1", "row"))
    return jax.shard_map(
        per_device,
        mesh=torus,
        in_specs=(P(None, CTR_ROW), P(None, CTR_ROW), P(None, CTR_ROW), P(None, CTR_ROW), P(), P()),
        out_specs=(P(None, CTR_ROW), P(None, CTR_ROW)),
        check_vma=False,
    )
```

profile of v0, /device:TPU:1, one launch (start us, length us, event | category | flops | bytes accessed | tf_op | source)
XLA Modules:
  0.0 825.5 jit_solution(6638212859591599418)
XLA Ops:
  10.1 9.2 %gather_fusion.2 = bf16[2048,440]{1,0:T(8,128)(2,1)} fusion(bf16[440,512]{0,1:T(8,128)(2,1)S(1)} %copy.46, s32[2048]{0:T(1024)S(1)} %fusion.56), kind=kCustom, calls=%fused_computation.clone | custom fusion | bytes 3612672 | tf_op jit(solution)/shard_map/jit(_take)/gather | solution.py:90
  23.3 5.5 gather_fusion.3
  29.0 7.6 gather_fusion.5
  36.7 7.6 gather_fusion.4
  48.3 10.0 %all-to-all-start = ((f32[16,128,128]{1,2,0:T(8,128)}), f32[16,128,128]{1,2,0:T(8,128)S(1)}, u32[]{:S(2)}, u32[]{:S(2)}) async-start(f32[16,128,128]{1,2,0:T(8,128)} %bitcast.9), calls=%async_computation.2 | async-start | bytes 2097152 | tf_op jit(solution)/shard_map/all_to_all | solution.py:30
  58.3 12.9 %reduce-scatter.5.cloned.1.call-done = bf16[440,256]{0,1:T(8,128)(2,1)} async-done(((bf16[440,2048]{0,1:T(8,128)(2,1)}), bf16[440,256]{0,1:T(8,128)(2,1)}) %reduce-scatter.5.cloned.1.call-update) | async-done | bytes 225296 | tf_op jit(solution)/shard_map/reduce_scatter | solution.py:19
  71.2 16.6 %all-to-all-done = f32[16,128,128]{1,2,0:T(8,128)S(1)} async-done(((f32[16,128,128]{1,2,0:T(8,128)}), f32[16,128,128]{1,2,0:T(8,128)S(1)}, u32[]{:S(2)}, u32[]{:S(2)}) %all-to-all-start) | async-done | bytes 1048608 | tf_op jit(solution)/shard_map/all_to_all | solution.py:30
  87.8 9.0 %reduce-scatter.7.cloned.1.call-done = bf16[440,128]{0,1:T(8,128)(2,1)} async-done(((bf16[440,256]{0,1:T(8,128)(2,1)}), bf16[440,128]{0,1:T(8,128)(2,1)}) %reduce-scatter.7.cloned.1.call-update) | async-done | bytes 112656 | tf_op jit(solution)/shard_map/reduce_scatter | solution.py:19
  97.9 15.1 %all_to_all.50 = f32[16,568,8]{1,2,0:T(8,128)S(1)} all-to-all(f32[16,568,8]{1,2,0:T(8,128)S(1)} %maximum_bitcast_fusion), channel_id=1, replica_groups=mesh['ctr_0'=8,'ctr_1'=2,'row'=16] {'row'}, dimensions={0} | all-to-all | bytes 581632 | tf_op jit(solution)/shard_map/all_to_all | solution.py:30
  113.0 10.7 %all_to_all.51 = f32[16,568,8]{1,2,0:T(8,128)S(1)} all-to-all(f32[16,568,8]{1,2,0:T(8,128)S(1)} %broadcast_in_dim.109), channel_id=1, replica_groups=mesh['ctr_0'=8,'ctr_1'=2,'row'=16] {'row'}, dimensions={0} | all-to-all | bytes 581632 | tf_op jit(solution)/shard_map/all_to_all | solution.py:42
  126.0 9.5 %all-to-all-start.3 = ((bf16[16,440,128]{2,1,0:T(8,128)(2,1)}), bf16[16,440,128]{2,1,0:T(8,128)(2,1)S(1)}, u32[]{:S(2)}, u32[]{:S(2)}) async-start(bf16[16,440,128]{2,1,0:T(8,128)(2,1)} %broadcast_in_dim.110), calls=%async_computation.5 | async-start | bytes 3604480 | tf_op jit(solution)/shard_map/all_to_all | solution.py:42
  136.4 9.2 %gather_fusion.6 = bf16[2048,440]{1,0:T(8,128)(2,1)} fusion(bf16[440,512]{0,1:T(8,128)(2,1)S(1)} %copy.46, s32[2048]{0:T(1024)S(1)} %fusion.57), kind=kCustom, calls=%fused_computation.2.clone | custom fusion | bytes 3612672 | tf_op jit(solution)/shard_map/jit(_take)/gather | solution.py:90
  149.7 35.5 %all-to-all-done.3 = bf16[16,440,128]{2,1,0:T(8,128)(2,1)S(1)} async-done(((bf16[16,440,128]{2,1,0:T(8,128)(2,1)}), bf16[16,440,128]{2,1,0:T(8,128)(2,1)S(1)}, u32[]{:S(2)}, u32[]{:S(2)}) %all-to-all-start.3) | async-done | bytes 1802272 | tf_op jit(solution)/shard_map/all_to_all | solution.py:42
  188.7 11.7 %cholesky.44 = f32[128,128]{1,0:T(8,128)S(1)} custom-call(f32[128,128]{1,0:T(8,128)S(1)} %fusion.55), custom_call_target="Cholesky" | custom-call | tf_op jit(solution)/shard_map/jit(cholesky)/cholesky | solution.py:66
  201.8 9.8 %custom-call.10 = f32[1,128,128]{1,2,0:T(8,128)S(1)} custom-call(f32[1,128,128]{2,1,0:T(8,128)S(1)} %fusion.46), custom_call_target="InvertDiagBlocksLowerTriangular" | custom-call | tf_op jit(solution)/shard_map/jit(_cho_solve)/triangular_solve | solution.py:67
  212.5 164.0 %while.32 = (s32[]{:T(128)}, bf16[128,2048]{1,0:T(8,128)(2,1)S(1)}, bf16[128,128]{1,0:T(8,128)(2,1)S(1)}, s32[]{:T(128)}, bf16[2048,128]{1,0:T(8,128)(2,1)S(1)},...) while((s32[]{:T(128)}, bf16[128,2048]{1,0:T(8,128)(2,1)S(1)}, ...), condition=%wide.region_7.12_spmd.clone, body=%wide.region_6.11_spmd.clone.sunk | while | flops 92356616 | bytes 4587739 | solution.py:128
  214.9 6.1 collective-permute-done
  226.0 6.1 collective-permute-done
  237.1 6.1 collective-permute-done
  248.2 6.1 collective-permute-done
  259.3 6.1 collective-permute-done
  270.4 6.1 collective-permute-done
  281.5 6.1 collective-permute-done
  292.6 6.1 collective-permute-done
  303.7 6.1 collective-permute-done
  314.8 6.1 collective-permute-done
  325.9 6.1 collective-permute-done
  337.0 6.1 collective-permute-done
  348.1 6.1 collective-permute-done
  359.2 6.1 collective-permute-done
  370.4 6.1 collective-permute-done
  378.1 26.2 %all-to-all-start.4 = ((bf16[16,128,128]{1,2,0:T(8,128)(2,1)}), bf16[16,128,128]{1,2,0:T(8,128)(2,1)S(1)}, u32[]{:S(2)}, u32[]{:S(2)}) async-start(bf16[16,128,128]{1,2,0:T(8,128)(2,1)} %broadcast_in_dim.111), calls=%async_computation.6 | async-start | bytes 1048576 | tf_op jit(solution)/shard_map/all_to_all | solution.py:42
  404.3 7.6 gather_fusion.7
  411.9 9.6 %all-to-all-done.4 = bf16[16,128,128]{1,2,0:T(8,128)(2,1)S(1)} async-done(((bf16[16,128,128]{1,2,0:T(8,128)(2,1)}), bf16[16,128,128]{1,2,0:T(8,128)(2,1)S(1)}, u32[]{:S(2)}, u32[]{:S(2)}) %all-to-all-start.4) | async-done | bytes 524320 | tf_op jit(solution)/shard_map/all_to_all | solution.py:42
  421.5 15.4 %scatter_custom_fusion = f32[128,512]{0,1:T(8,128)S(1)} fusion(f32[128,512]{0,1:T(8,128)S(1)} %copy.49, s32[2048]{0:T(1024)S(1)} %bitcast.207, bf16[128,2048]{0,1:T(8,128)(2,1)S(1)} %bitcast.196, f32[]{:T(128)} %constant.156.clone.1, pred[2048]{0:T(1024)(128)(4,1)S(1)} %and_bitcast_fusion.1), kind=kCustom, calls=%fused_computation.51 | custom fusion | flops 786432 | bytes 788484 | tf_op jit(solution)/shard_map/scatter-add | solution.py:135
  436.9 7.6 gather_fusion.9
  449.2 7.6 gather_fusion.8
  464.7 11.7 %reduce-scatter.11.cloned.1.call-done = bf16[440,128]{0,1:T(8,128)(2,1)} async-done(((bf16[440,256]{0,1:T(8,128)(2,1)}), bf16[440,128]{0,1:T(8,128)(2,1)}) %reduce-scatter.11.cloned.1.call-update) | async-done | bytes 112656 | tf_op jit(solution)/shard_map/reduce_scatter | solution.py:19
  477.4 14.0 %all-to-all-done.5 = f32[16,128,128]{1,2,0:T(8,128)S(1)} async-done(((f32[16,128,128]{1,2,0:T(8,128)}), f32[16,128,128]{1,2,0:T(8,128)S(1)}, u32[]{:S(2)}, u32[]{:S(2)}) %all-to-all-start.5) | async-done | bytes 1048608 | tf_op jit(solution)/shard_map/all_to_all | solution.py:30
  491.5 11.8 %all_to_all.52 = f32[16,568,8]{1,2,0:T(8,128)S(1)} all-to-all(f32[16,568,8]{1,2,0:T(8,128)S(1)} %maximum_bitcast_fusion.1), channel_id=1, replica_groups=mesh['ctr_0'=8,'ctr_1'=2,'row'=16] {'row'}, dimensions={0} | all-to-all | bytes 581632 | tf_op jit(solution)/shard_map/all_to_all | solution.py:30
  503.4 11.4 %all_to_all.53 = f32[16,568,8]{1,2,0:T(8,128)S(1)} all-to-all(f32[16,568,8]{1,2,0:T(8,128)S(1)} %broadcast_in_dim.114), channel_id=1, replica_groups=mesh['ctr_0'=8,'ctr_1'=2,'row'=16] {'row'}, dimensions={0} | all-to-all | bytes 581632 | tf_op jit(solution)/shard_map/all_to_all | solution.py:42
  516.4 5.1 all-to-all-start.8
  521.7 43.0 %all-to-all-done.8 = bf16[16,440,128]{2,1,0:T(8,128)(2,1)S(1)} async-done(((bf16[16,440,128]{2,1,0:T(8,128)(2,1)}), bf16[16,440,128]{2,1,0:T(8,128)(2,1)S(1)}, u32[]{:S(2)}, u32[]{:S(2)}) %all-to-all-start.8) | async-done | bytes 1802272 | tf_op jit(solution)/shard_map/all_to_all | solution.py:42
  567.9 11.7 %cholesky.55 = f32[128,128]{1,0:T(8,128)S(1)} custom-call(f32[128,128]{1,0:T(8,128)S(1)} %fusion.51), custom_call_target="Cholesky" | custom-call | tf_op jit(solution)/shard_map/jit(cholesky)/cholesky | solution.py:66
  581.0 9.8 %custom-call.11 = f32[1,128,128]{1,2,0:T(8,128)S(1)} custom-call(f32[1,128,128]{2,1,0:T(8,128)S(1)} %fusion.47), custom_call_target="InvertDiagBlocksLowerTriangular" | custom-call | tf_op jit(solution)/shard_map/jit(_cho_solve)/triangular_solve | solution.py:67
  591.6 164.0 %while.33 = (s32[]{:T(128)}, bf16[128,2048]{1,0:T(8,128)(2,1)S(1)}, bf16[128,128]{1,0:T(8,128)(2,1)S(1)}, s32[]{:T(128)}, bf16[2048,128]{1,0:T(8,128)(2,1)S(1)},...) while((s32[]{:T(128)}, bf16[128,2048]{1,0:T(8,128)(2,1)S(1)}, ...), condition=%wide.region_14.19_spmd.clone, body=%wide.region_13.18_spmd.clone.sunk | while | flops 92356616 | bytes 4587739 | solution.py:128
  594.1 6.1 collective-permute-done.1
  605.2 6.1 collective-permute-done.1
  616.3 6.1 collective-permute-done.1
  627.4 6.1 collective-permute-done.1
  638.5 6.1 collective-permute-done.1
  649.6 6.1 collective-permute-done.1
  660.7 6.1 collective-permute-done.1
  671.8 6.1 collective-permute-done.1
  682.9 6.1 collective-permute-done.1
  694.0 6.1 collective-permute-done.1
  705.1 6.1 collective-permute-done.1
  716.2 6.1 collective-permute-done.1
  727.3 6.1 collective-permute-done.1
  738.4 6.1 collective-permute-done.1
  749.5 6.1 collective-permute-done.1
  757.2 25.0 %all-to-all-start.9 = ((bf16[16,128,128]{1,2,0:T(8,128)(2,1)}), bf16[16,128,128]{1,2,0:T(8,128)(2,1)S(1)}, u32[]{:S(2)}, u32[]{:S(2)}) async-start(bf16[16,128,128]{1,2,0:T(8,128)(2,1)} %broadcast_in_dim.116), calls=%async_computation.13 | async-start | bytes 1048576 | tf_op jit(solution)/shard_map/all_to_all | solution.py:42
  782.3 17.2 %all-to-all-done.9 = bf16[16,128,128]{1,2,0:T(8,128)(2,1)S(1)} async-done(((bf16[16,128,128]{1,2,0:T(8,128)(2,1)}), bf16[16,128,128]{1,2,0:T(8,128)(2,1)S(1)}, u32[]{:S(2)}, u32[]{:S(2)}) %all-to-all-start.9) | async-done | bytes 524320 | tf_op jit(solution)/shard_map/all_to_all | solution.py:42
  799.5 15.0 %scatter_custom_fusion.1 = f32[128,512]{0,1:T(8,128)S(1)} fusion(f32[128,512]{0,1:T(8,128)S(1)} %scatter_custom_fusion, s32[2048]{0:T(1024)S(1)} %bitcast.206, bf16[128,2048]{0,1:T(8,128)(2,1)S(1)} %bitcast.194, f32[]{:T(128)} %constant.156.clone.1, pred[2048]{0:T(1024)(128)(4,1)S(1)} %and_bitcast_fusion), kind=kCustom, calls=%fused_computation.46 | custom fusion | flops 786432 | bytes 788484 | tf_op jit(solution)/shard_map/scatter-add | solution.py:135
  (238 shorter events, 196.8 us)
Async XLA Ops:
  7.2 1.1 copy-start
  7.2 64.0 %reduce-scatter.5.cloned.1.call-start = ((), (), s32[]{:S(2)}) async-start(), calls=%async_computation.14 | async-start | bytes 2359296 | tf_op jit(solution)/shard_map/reduce_scatter | solution.py:19
  22.2 0.9 copy-start.12
  23.3 5.5 copy-start.13
  28.9 7.6 copy-start.14
  48.3 39.5 %all-to-all-start = ((f32[16,128,128]{1,2,0:T(8,128)}), f32[16,128,128]{1,2,0:T(8,128)S(1)}, u32[]{:S(2)}, u32[]{:S(2)}) async-start(f32[16,128,128]{1,2,0:T(8,128)} %bitcast.9), calls=%async_computation.2 | async-start | bytes 2097152 | tf_op jit(solution)/shard_map/all_to_all | solution.py:30
  58.3 38.6 %reduce-scatter.7.cloned.1.call-start = ((), (), s32[]{:S(2)}) async-start(), calls=%async_computation.15 | async-start | bytes 393216 | tf_op jit(solution)/shard_map/reduce_scatter | solution.py:19
  123.7 0.7 copy-start.9
  126.0 59.1 %all-to-all-start.3 = ((bf16[16,440,128]{2,1,0:T(8,128)(2,1)}), bf16[16,440,128]{2,1,0:T(8,128)(2,1)S(1)}, u32[]{:S(2)}, u32[]{:S(2)}) async-start(bf16[16,440,128]{2,1,0:T(8,128)(2,1)} %broadcast_in_dim.110), calls=%async_computation.5 | async-start | bytes 3604480 | tf_op jit(solution)/shard_map/all_to_all | solution.py:42
  135.6 328.7 %reduce-scatter.9.cloned.1.call-start = ((), (), s32[]{:S(2)}) async-start(), calls=%async_computation.16 | async-start | bytes 2359296 | tf_op jit(solution)/shard_map/reduce_scatter | solution.py:19
  185.1 1.6 copy-start.1
  186.8 1.0 copy-start.11
  186.8 25.3 %copy-start.5 = (bf16[2048,128]{0,1:T(8,128)(2,1)}, bf16[2048,128]{0,1:T(8,128)(2,1)S(1)}, u32[]{:S(2)}) copy-start(bf16[2048,128]{0,1:T(8,128)(2,1)S(1)} %get-tuple-element.394) | copy-start | bytes 1572868
  212.5 164.1 %copy-start.6 = (bf16[2048,128]{0,1:T(8,128)(2,1)S(1)}, bf16[2048,128]{0,1:T(8,128)(2,1)}, u32[]{:S(2)}) copy-start(bf16[2048,128]{0,1:T(8,128)(2,1)} %copy-done.5) | copy-start | bytes 1572868
  213.0 8.0 collective-permute-start
  221.6 10.5 %collective-permute-start = (bf16[128,2048]{1,0:T(8,128)(2,1)S(1)}, bf16[128,2048]{1,0:T(8,128)(2,1)S(1)}, u32[]{:S(2)}, u32[]{:S(2)}) collective-permute-start(bf16[128,2048]{1,0:T(8,128)(2,1)S(1)} %get-tuple-element.483), channel_id=1, source_target_pairs={{0,16},{16,32},{32,48},{48,64},{64,80},{80,96},{96,112},{112,128},... | collective-permute-start | bytes 1572872 | tf_op jit(solution)/shard_map/while/body/eval_jaxpr/ppermute | solution.py:54
  232.7 10.5 %collective-permute-start = (bf16[128,2048]{1,0:T(8,128)(2,1)S(1)}, bf16[128,2048]{1,0:T(8,128)(2,1)S(1)}, u32[]{:S(2)}, u32[]{:S(2)}) collective-permute-start(bf16[128,2048]{1,0:T(8,128)(2,1)S(1)} %get-tuple-element.483), channel_id=1, source_target_pairs={{0,16},{16,32},{32,48},{48,64},{64,80},{80,96},{96,112},{112,128},... | collective-permute-start | bytes 1572872 | tf_op jit(solution)/shard_map/while/body/eval_jaxpr/ppermute | solution.py:54
  243.8 10.5 %collective-permute-start = (bf16[128,2048]{1,0:T(8,128)(2,1)S(1)}, bf16[128,2048]{1,0:T(8,128)(2,1)S(1)}, u32[]{:S(2)}, u32[]{:S(2)}) collective-permute-start(bf16[128,2048]{1,0:T(8,128)(2,1)S(1)} %get-tuple-element.483), channel_id=1, source_target_pairs={{0,16},{16,32},{32,48},{48,64},{64,80},{80,96},{96,112},{112,128},... | collective-permute-start | bytes 1572872 | tf_op jit(solution)/shard_map/while/body/eval_jaxpr/ppermute | solution.py:54
  254.9 10.5 %collective-permute-start = (bf16[128,2048]{1,0:T(8,128)(2,1)S(1)}, bf16[128,2048]{1,0:T(8,128)(2,1)S(1)}, u32[]{:S(2)}, u32[]{:S(2)}) collective-permute-start(bf16[128,2048]{1,0:T(8,128)(2,1)S(1)} %get-tuple-element.483), channel_id=1, source_target_pairs={{0,16},{16,32},{32,48},{48,64},{64,80},{80,96},{96,112},{112,128},... | collective-permute-start | bytes 1572872 | tf_op jit(solution)/shard_map/while/body/eval_jaxpr/ppermute | solution.py:54
  266.0 10.5 %collective-permute-start = (bf16[128,2048]{1,0:T(8,128)(2,1)S(1)}, bf16[128,2048]{1,0:T(8,128)(2,1)S(1)}, u32[]{:S(2)}, u32[]{:S(2)}) collective-permute-start(bf16[128,2048]{1,0:T(8,128)(2,1)S(1)} %get-tuple-element.483), channel_id=1, source_target_pairs={{0,16},{16,32},{32,48},{48,64},{64,80},{80,96},{96,112},{112,128},... | collective-permute-start | bytes 1572872 | tf_op jit(solution)/shard_map/while/body/eval_jaxpr/ppermute | solution.py:54
  277.1 10.5 %collective-permute-start = (bf16[128,2048]{1,0:T(8,128)(2,1)S(1)}, bf16[128,2048]{1,0:T(8,128)(2,1)S(1)}, u32[]{:S(2)}, u32[]{:S(2)}) collective-permute-start(bf16[128,2048]{1,0:T(8,128)(2,1)S(1)} %get-tuple-element.483), channel_id=1, source_target_pairs={{0,16},{16,32},{32,48},{48,64},{64,80},{80,96},{96,112},{112,128},... | collective-permute-start | bytes 1572872 | tf_op jit(solution)/shard_map/while/body/eval_jaxpr/ppermute | solution.py:54
  288.2 10.5 %collective-permute-start = (bf16[128,2048]{1,0:T(8,128)(2,1)S(1)}, bf16[128,2048]{1,0:T(8,128)(2,1)S(1)}, u32[]{:S(2)}, u32[]{:S(2)}) collective-permute-start(bf16[128,2048]{1,0:T(8,128)(2,1)S(1)} %get-tuple-element.483), channel_id=1, source_target_pairs={{0,16},{16,32},{32,48},{48,64},{64,80},{80,96},{96,112},{112,128},... | collective-permute-start | bytes 1572872 | tf_op jit(solution)/shard_map/while/body/eval_jaxpr/ppermute | solution.py:54
  299.3 10.5 %collective-permute-start = (bf16[128,2048]{1,0:T(8,128)(2,1)S(1)}, bf16[128,2048]{1,0:T(8,128)(2,1)S(1)}, u32[]{:S(2)}, u32[]{:S(2)}) collective-permute-start(bf16[128,2048]{1,0:T(8,128)(2,1)S(1)} %get-tuple-element.483), channel_id=1, source_target_pairs={{0,16},{16,32},{32,48},{48,64},{64,80},{80,96},{96,112},{112,128},... | collective-permute-start | bytes 1572872 | tf_op jit(solution)/shard_map/while/body/eval_jaxpr/ppermute | solution.py:54
  310.4 10.5 %collective-permute-start = (bf16[128,2048]{1,0:T(8,128)(2,1)S(1)}, bf16[128,2048]{1,0:T(8,128)(2,1)S(1)}, u32[]{:S(2)}, u32[]{:S(2)}) collective-permute-start(bf16[128,2048]{1,0:T(8,128)(2,1)S(1)} %get-tuple-element.483), channel_id=1, source_target_pairs={{0,16},{16,32},{32,48},{48,64},{64,80},{80,96},{96,112},{112,128},... | collective-permute-start | bytes 1572872 | tf_op jit(solution)/shard_map/while/body/eval_jaxpr/ppermute | solution.py:54
  321.5 10.5 %collective-permute-start = (bf16[128,2048]{1,0:T(8,128)(2,1)S(1)}, bf16[128,2048]{1,0:T(8,128)(2,1)S(1)}, u32[]{:S(2)}, u32[]{:S(2)}) collective-permute-start(bf16[128,2048]{1,0:T(8,128)(2,1)S(1)} %get-tuple-element.483), channel_id=1, source_target_pairs={{0,16},{16,32},{32,48},{48,64},{64,80},{80,96},{96,112},{112,128},... | collective-permute-start | bytes 1572872 | tf_op jit(solution)/shard_map/while/body/eval_jaxpr/ppermute | solution.py:54
  332.6 10.5 %collective-permute-start = (bf16[128,2048]{1,0:T(8,128)(2,1)S(1)}, bf16[128,2048]{1,0:T(8,128)(2,1)S(1)}, u32[]{:S(2)}, u32[]{:S(2)}) collective-permute-start(bf16[128,2048]{1,0:T(8,128)(2,1)S(1)} %get-tuple-element.483), channel_id=1, source_target_pairs={{0,16},{16,32},{32,48},{48,64},{64,80},{80,96},{96,112},{112,128},... | collective-permute-start | bytes 1572872 | tf_op jit(solution)/shard_map/while/body/eval_jaxpr/ppermute | solution.py:54
  343.7 10.5 %collective-permute-start = (bf16[128,2048]{1,0:T(8,128)(2,1)S(1)}, bf16[128,2048]{1,0:T(8,128)(2,1)S(1)}, u32[]{:S(2)}, u32[]{:S(2)}) collective-permute-start(bf16[128,2048]{1,0:T(8,128)(2,1)S(1)} %get-tuple-element.483), channel_id=1, source_target_pairs={{0,16},{16,32},{32,48},{48,64},{64,80},{80,96},{96,112},{112,128},... | collective-permute-start | bytes 1572872 | tf_op jit(solution)/shard_map/while/body/eval_jaxpr/ppermute | solution.py:54
  354.9 10.5 %collective-permute-start = (bf16[128,2048]{1,0:T(8,128)(2,1)S(1)}, bf16[128,2048]{1,0:T(8,128)(2,1)S(1)}, u32[]{:S(2)}, u32[]{:S(2)}) collective-permute-start(bf16[128,2048]{1,0:T(8,128)(2,1)S(1)} %get-tuple-element.483), channel_id=1, source_target_pairs={{0,16},{16,32},{32,48},{48,64},{64,80},{80,96},{96,112},{112,128},... | collective-permute-start | bytes 1572872 | tf_op jit(solution)/shard_map/while/body/eval_jaxpr/ppermute | solution.py:54
  366.0 10.5 %collective-permute-start = (bf16[128,2048]{1,0:T(8,128)(2,1)S(1)}, bf16[128,2048]{1,0:T(8,128)(2,1)S(1)}, u32[]{:S(2)}, u32[]{:S(2)}) collective-permute-start(bf16[128,2048]{1,0:T(8,128)(2,1)S(1)} %get-tuple-element.483), channel_id=1, source_target_pairs={{0,16},{16,32},{32,48},{48,64},{64,80},{80,96},{96,112},{112,128},... | collective-permute-start | bytes 1572872 | tf_op jit(solution)/shard_map/while/body/eval_jaxpr/ppermute | solution.py:54
  378.1 43.4 %all-to-all-start.4 = ((bf16[16,128,128]{1,2,0:T(8,128)(2,1)}), bf16[16,128,128]{1,2,0:T(8,128)(2,1)S(1)}, u32[]{:S(2)}, u32[]{:S(2)}) async-start(bf16[16,128,128]{1,2,0:T(8,128)(2,1)} %broadcast_in_dim.111), calls=%async_computation.6 | async-start | bytes 1048576 | tf_op jit(solution)/shard_map/all_to_all | solution.py:42
  436.9 7.7 copy-start.2
  436.9 7.7 copy-start.15
  449.2 7.6 copy-start.7
  449.2 7.6 copy-start.8
  460.6 30.7 %all-to-all-start.5 = ((f32[16,128,128]{1,2,0:T(8,128)}), f32[16,128,128]{1,2,0:T(8,128)S(1)}, u32[]{:S(2)}, u32[]{:S(2)}) async-start(f32[16,128,128]{1,2,0:T(8,128)} %bitcast.34), calls=%async_computation.9 | async-start | bytes 2097152 | tf_op jit(solution)/shard_map/all_to_all | solution.py:30
  464.2 12.3 %reduce-scatter.11.cloned.1.call-start = ((), (), s32[]{:S(2)}) async-start(), calls=%async_computation.17 | async-start | bytes 393216 | tf_op jit(solution)/shard_map/reduce_scatter | solution.py:19
  516.4 48.3 %all-to-all-start.8 = ((bf16[16,440,128]{2,1,0:T(8,128)(2,1)}), bf16[16,440,128]{2,1,0:T(8,128)(2,1)S(1)}, u32[]{:S(2)}, u32[]{:S(2)}) async-start(bf16[16,440,128]{2,1,0:T(8,128)(2,1)} %broadcast_in_dim.115), calls=%async_computation.12 | async-start | bytes 3604480 | tf_op jit(solution)/shard_map/all_to_all | solution.py:42
  564.7 1.2 copy-start.3
  565.9 1.0 copy-start.10
  592.2 8.0 collective-permute-start.1
  600.8 10.5 %collective-permute-start.1 = (bf16[128,2048]{1,0:T(8,128)(2,1)S(1)}, bf16[128,2048]{1,0:T(8,128)(2,1)S(1)}, u32[]{:S(2)}, u32[]{:S(2)}) collective-permute-start(bf16[128,2048]{1,0:T(8,128)(2,1)S(1)} %get-tuple-element.492), channel_id=1, source_target_pairs={{0,16},{16,32},{32,48},{48,64},{64,80},{80,96},{96,112},{112,128},... | collective-permute-start | bytes 1572872 | tf_op jit(solution)/shard_map/while/body/eval_jaxpr/ppermute | solution.py:54
  611.9 10.5 %collective-permute-start.1 = (bf16[128,2048]{1,0:T(8,128)(2,1)S(1)}, bf16[128,2048]{1,0:T(8,128)(2,1)S(1)}, u32[]{:S(2)}, u32[]{:S(2)}) collective-permute-start(bf16[128,2048]{1,0:T(8,128)(2,1)S(1)} %get-tuple-element.492), channel_id=1, source_target_pairs={{0,16},{16,32},{32,48},{48,64},{64,80},{80,96},{96,112},{112,128},... | collective-permute-start | bytes 1572872 | tf_op jit(solution)/shard_map/while/body/eval_jaxpr/ppermute | solution.py:54
  623.0 10.5 %collective-permute-start.1 = (bf16[128,2048]{1,0:T(8,128)(2,1)S(1)}, bf16[128,2048]{1,0:T(8,128)(2,1)S(1)}, u32[]{:S(2)}, u32[]{:S(2)}) collective-permute-start(bf16[128,2048]{1,0:T(8,128)(2,1)S(1)} %get-tuple-element.492), channel_id=1, source_target_pairs={{0,16},{16,32},{32,48},{48,64},{64,80},{80,96},{96,112},{112,128},... | collective-permute-start | bytes 1572872 | tf_op jit(solution)/shard_map/while/body/eval_jaxpr/ppermute | solution.py:54
  634.1 10.5 %collective-permute-start.1 = (bf16[128,2048]{1,0:T(8,128)(2,1)S(1)}, bf16[128,2048]{1,0:T(8,128)(2,1)S(1)}, u32[]{:S(2)}, u32[]{:S(2)}) collective-permute-start(bf16[128,2048]{1,0:T(8,128)(2,1)S(1)} %get-tuple-element.492), channel_id=1, source_target_pairs={{0,16},{16,32},{32,48},{48,64},{64,80},{80,96},{96,112},{112,128},... | collective-permute-start | bytes 1572872 | tf_op jit(solution)/shard_map/while/body/eval_jaxpr/ppermute | solution.py:54
  645.2 10.5 %collective-permute-start.1 = (bf16[128,2048]{1,0:T(8,128)(2,1)S(1)}, bf16[128,2048]{1,0:T(8,128)(2,1)S(1)}, u32[]{:S(2)}, u32[]{:S(2)}) collective-permute-start(bf16[128,2048]{1,0:T(8,128)(2,1)S(1)} %get-tuple-element.492), channel_id=1, source_target_pairs={{0,16},{16,32},{32,48},{48,64},{64,80},{80,96},{96,112},{112,128},... | collective-permute-start | bytes 1572872 | tf_op jit(solution)/shard_map/while/body/eval_jaxpr/ppermute | solution.py:54
  656.3 10.5 %collective-permute-start.1 = (bf16[128,2048]{1,0:T(8,128)(2,1)S(1)}, bf16[128,2048]{1,0:T(8,128)(2,1)S(1)}, u32[]{:S(2)}, u32[]{:S(2)}) collective-permute-start(bf16[128,2048]{1,0:T(8,128)(2,1)S(1)} %get-tuple-element.492), channel_id=1, source_target_pairs={{0,16},{16,32},{32,48},{48,64},{64,80},{80,96},{96,112},{112,128},... | collective-permute-start | bytes 1572872 | tf_op jit(solution)/shard_map/while/body/eval_jaxpr/ppermute | solution.py:54
  667.4 10.5 %collective-permute-start.1 = (bf16[128,2048]{1,0:T(8,128)(2,1)S(1)}, bf16[128,2048]{1,0:T(8,128)(2,1)S(1)}, u32[]{:S(2)}, u32[]{:S(2)}) collective-permute-start(bf16[128,2048]{1,0:T(8,128)(2,1)S(1)} %get-tuple-element.492), channel_id=1, source_target_pairs={{0,16},{16,32},{32,48},{48,64},{64,80},{80,96},{96,112},{112,128},... | collective-permute-start | bytes 1572872 | tf_op jit(solution)/shard_map/while/body/eval_jaxpr/ppermute | solution.py:54
  678.5 10.5 %collective-permute-start.1 = (bf16[128,2048]{1,0:T(8,128)(2,1)S(1)}, bf16[128,2048]{1,0:T(8,128)(2,1)S(1)}, u32[]{:S(2)}, u32[]{:S(2)}) collective-permute-start(bf16[128,2048]{1,0:T(8,128)(2,1)S(1)} %get-tuple-element.492), channel_id=1, source_target_pairs={{0,16},{16,32},{32,48},{48,64},{64,80},{80,96},{96,112},{112,128},... | collective-permute-start | bytes 1572872 | tf_op jit(solution)/shard_map/while/body/eval_jaxpr/ppermute | solution.py:54
  689.6 10.5 %collective-permute-start.1 = (bf16[128,2048]{1,0:T(8,128)(2,1)S(1)}, bf16[128,2048]{1,0:T(8,128)(2,1)S(1)}, u32[]{:S(2)}, u32[]{:S(2)}) collective-permute-start(bf16[128,2048]{1,0:T(8,128)(2,1)S(1)} %get-tuple-element.492), channel_id=1, source_target_pairs={{0,16},{16,32},{32,48},{48,64},{64,80},{80,96},{96,112},{112,128},... | collective-permute-start | bytes 1572872 | tf_op jit(solution)/shard_map/while/body/eval_jaxpr/ppermute | solution.py:54
  700.7 10.5 %collective-permute-start.1 = (bf16[128,2048]{1,0:T(8,128)(2,1)S(1)}, bf16[128,2048]{1,0:T(8,128)(2,1)S(1)}, u32[]{:S(2)}, u32[]{:S(2)}) collective-permute-start(bf16[128,2048]{1,0:T(8,128)(2,1)S(1)} %get-tuple-element.492), channel_id=1, source_target_pairs={{0,16},{16,32},{32,48},{48,64},{64,80},{80,96},{96,112},{112,128},... | collective-permute-start | bytes 1572872 | tf_op jit(solution)/shard_map/while/body/eval_jaxpr/ppermute | solution.py:54
  711.8 10.5 %collective-permute-start.1 = (bf16[128,2048]{1,0:T(8,128)(2,1)S(1)}, bf16[128,2048]{1,0:T(8,128)(2,1)S(1)}, u32[]{:S(2)}, u32[]{:S(2)}) collective-permute-start(bf16[128,2048]{1,0:T(8,128)(2,1)S(1)} %get-tuple-element.492), channel_id=1, source_target_pairs={{0,16},{16,32},{32,48},{48,64},{64,80},{80,96},{96,112},{112,128},... | collective-permute-start | bytes 1572872 | tf_op jit(solution)/shard_map/while/body/eval_jaxpr/ppermute | solution.py:54
  722.9 10.5 %collective-permute-start.1 = (bf16[128,2048]{1,0:T(8,128)(2,1)S(1)}, bf16[128,2048]{1,0:T(8,128)(2,1)S(1)}, u32[]{:S(2)}, u32[]{:S(2)}) collective-permute-start(bf16[128,2048]{1,0:T(8,128)(2,1)S(1)} %get-tuple-element.492), channel_id=1, source_target_pairs={{0,16},{16,32},{32,48},{48,64},{64,80},{80,96},{96,112},{112,128},... | collective-permute-start | bytes 1572872 | tf_op jit(solution)/shard_map/while/body/eval_jaxpr/ppermute | solution.py:54
  734.0 10.5 %collective-permute-start.1 = (bf16[128,2048]{1,0:T(8,128)(2,1)S(1)}, bf16[128,2048]{1,0:T(8,128)(2,1)S(1)}, u32[]{:S(2)}, u32[]{:S(2)}) collective-permute-start(bf16[128,2048]{1,0:T(8,128)(2,1)S(1)} %get-tuple-element.492), channel_id=1, source_target_pairs={{0,16},{16,32},{32,48},{48,64},{64,80},{80,96},{96,112},{112,128},... | collective-permute-start | bytes 1572872 | tf_op jit(solution)/shard_map/while/body/eval_jaxpr/ppermute | solution.py:54
  745.1 10.5 %collective-permute-start.1 = (bf16[128,2048]{1,0:T(8,128)(2,1)S(1)}, bf16[128,2048]{1,0:T(8,128)(2,1)S(1)}, u32[]{:S(2)}, u32[]{:S(2)}) collective-permute-start(bf16[128,2048]{1,0:T(8,128)(2,1)S(1)} %get-tuple-element.492), channel_id=1, source_target_pairs={{0,16},{16,32},{32,48},{48,64},{64,80},{80,96},{96,112},{112,128},... | collective-permute-start | bytes 1572872 | tf_op jit(solution)/shard_map/while/body/eval_jaxpr/ppermute | solution.py:54
  756.0 59.4 %copy-start.4 = (bf16[16,440,128]{2,1,0:T(8,128)(2,1)S(1)}, bf16[16,440,128]{2,1,0:T(8,128)(2,1)}, u32[]{:S(2)}) copy-start(bf16[16,440,128]{2,1,0:T(8,128)(2,1)} %copy-done.3) | copy-start | bytes 5406724
  757.2 42.2 %all-to-all-start.9 = ((bf16[16,128,128]{1,2,0:T(8,128)(2,1)}), bf16[16,128,128]{1,2,0:T(8,128)(2,1)S(1)}, u32[]{:S(2)}, u32[]{:S(2)}) async-start(bf16[16,128,128]{1,2,0:T(8,128)(2,1)} %broadcast_in_dim.116), calls=%async_computation.13 | async-start | bytes 1048576 | tf_op jit(solution)/shard_map/all_to_all | solution.py:42
Sparse Core Ops, SparseCore 0:
  22.4 48.7 reduce-scatter.4
  73.7 23.1 reduce-scatter.6
  148.7 52.1 reduce-scatter.8
  467.1 9.2 reduce-scatter.10
where the time goes:
time: 828 us; the launch traced here: 825 us
  waiting for transfers between devices  353 us (43%)
  starting transfers between devices  206 us (25%)
  other arithmetic  94.7 us (11%)
  local copies, waits for them, and re-layouts  79.8 us (10%)
  blocking collectives  49 us (6%)
  matrix products  26.6 us (3%)
  between operations  14.3 us (2%)
    ppermute x30, waiting for transfers between devices, from_behind(): return lax.ppermute(array, axis, pairs)  183 us
    ppermute x30, starting transfers between devices, from_behind(): return lax.ppermute(array, axis, pairs)  127 us
    all_to_all x4, waiting for transfers between devices, sent_to_all(): lax.all_to_all(jnp.broadcast_to(array[None], (size, *array.shape)), axis,...  105 us
    all_to_all x4, starting transfers between devices, sent_to_all(): lax.all_to_all(jnp.broadcast_to(array[None], (size, *array.shape)), axis,...  65.9 us
    reduce_scatter x4, waiting for transfers between devices, scatter_axes(): array = lax.psum_scatter(array, axis, scatter_dimension=dim, tiled=True)  33.6 us
    all_to_all x2, waiting for transfers between devices, sum_at_owner(): pieces = lax.all_to_all(split_up(array, dim, size), axis, 0, 0, tiled=True)  30.5 us
    scatter-add x2, other arithmetic, per_device(): coeffs.at[:, safe].add(jnp.where(keep, deltas.astype(jnp.float32), 0.0))  30.4 us
    all_to_all x2, blocking collectives, sum_at_owner(): pieces = lax.all_to_all(split_up(array, dim, size), axis, 0, 0, tiled=True)  26.9 us
  transfers between devices with their start and end apart: 40, of which 39 were waited for; matrix products, arithmetic and copies ran while one was open for 15% of the time, Pallas kernels for 0%

commit v1 on v0

v1 whole, which is shorter than its diff:
```python
import functools
import math

import jax
import jax.numpy as jnp
from jax import lax
from jax.experimental import pallas as pl
from jax.experimental.pallas import tpu as pltpu
from jax.sharding import Mesh
from jax.sharding import PartitionSpec as P

STEPS = 2
ALL = ("ctr_0", "ctr_1", "row")
F32 = jnp.float32
BF = jnp.bfloat16
ridge = 2.0
NT = (((1,), (1,)), ((), ()))
NN = (((1,), (0,)), ((), ()))
VMEM = pl.BlockSpec(memory_space=pltpu.VMEM)
SMEM = pl.BlockSpec(memory_space=pltpu.SMEM)


def dot(a, b, dims=NN):
    return lax.dot_general(a, b, dims, preferred_element_type=F32)


def split(x):
    hi = x.astype(BF)
    return hi, (x - hi.astype(F32)).astype(BF)


def pick_kernel(base_ref, ids_ref, x_ref, t_ref, p_ref, a_ref, out_ref, z_ref):
    outs = t_ref.shape[0]
    blocks, block = ids_ref.shape
    frames = x_ref.shape[1]
    hi, lo = split((t_ref[...] - p_ref[...] - ridge * a_ref[...]).T)
    z_ref[:, :outs] = hi
    z_ref[:, outs : 2 * outs] = lo
    z_ref[:, 2 * outs :] = x_ref[...].astype(F32).T.astype(BF)
    local = (ids_ref[...] - base_ref[0]).T
    lane = lax.broadcasted_iota(jnp.int32, (block, frames), 1)
    for j in range(blocks):
        hot = jnp.where(local[:, j : j + 1] == lane, 1.0, 0.0).astype(BF)
        out_ref[j * block : (j + 1) * block, :] = dot(hot, z_ref[...]).astype(BF)


def pick(base, ids, features, targets, predictions, coeffs):
    width = features.shape[0] + 2 * targets.shape[0]
    return pl.pallas_call(
        pick_kernel,
        out_shape=jax.ShapeDtypeStruct((ids.size, width), BF),
        in_specs=[SMEM, VMEM, VMEM, VMEM, VMEM, VMEM],
        out_specs=VMEM,
        scratch_shapes=[pltpu.VMEM((features.shape[1], width), BF)],
    )(base, ids, features, targets, predictions, coeffs)


def kernel_of(left, right, scale):
    return jnp.exp(scale * dot(left, right, NT))


def invert_direct(s_ref, x_ref, block):
    lane = lax.broadcasted_iota(jnp.int32, (block, block), 1)
    sub = lax.broadcasted_iota(jnp.int32, (block, block), 0)

    def one(b, _):
        def pivot(k, a):
            row = jnp.sum(jnp.where(sub == k, a, 0.0), axis=0, keepdims=True)
            col = jnp.sum(jnp.where(lane == k, a, 0.0), axis=1, keepdims=True)
            p = jnp.sum(jnp.where(lane[:1] == k, row, 0.0), axis=1, keepdims=True)
            inv = 1.0 / p
            rowp = jnp.where(lane[:1] == k, inv, row * inv)
            new = jnp.where(lane == k, 0.0, a) - col * rowp
            return jnp.where(sub == k, rowp, new)

        x_ref[b] = lax.fori_loop(0, block, pivot, s_ref[b])
        return 0

    lax.fori_loop(0, s_ref.shape[0], one, 0)


def invert_all(s_ref, sh_ref, sl_ref, x_ref, d_ref, block):
    nb = s_ref.shape[0]
    eye = lax.broadcasted_iota(jnp.int32, (block, block), 0) == lax.broadcasted_iota(
        jnp.int32, (block, block), 1
    )

    def start(b, _):
        s = s_ref[b]
        diag = jnp.where(eye, s, 0.0)
        dr = lax.rsqrt(jnp.sum(diag, axis=0, keepdims=True))
        dc = lax.rsqrt(jnp.sum(diag, axis=1, keepdims=True))
        s = s * dr * dc
        s_ref[b] = s
        d_ref[b] = dr * dc
        hi, lo = split(s)
        sh_ref[b] = hi
        sl_ref[b] = lo
        c = 1.0 / jnp.max(jnp.sum(jnp.abs(s), axis=1, keepdims=True), axis=0, keepdims=True)
        x_ref[b] = jnp.where(eye, 2.0 * c, 0.0) - (c * c) * s
        return 0

    lax.fori_loop(0, nb, start, 0)

    def settle(state):
        count, _ = state

        def one(b, worst):
            for u in range(4):
                i = 4 * b + u
                x = x_ref[i]
                xh, xl = split(x)
                y = dot(sh_ref[i], xl) + dot(sl_ref[i], xh) + dot(sh_ref[i], xh)
                r = jnp.where(eye, 1.0, 0.0) - y
                x_ref[i] = x + dot(xh, r.astype(BF))
                worst = jnp.maximum(worst, jnp.sum(r * r, axis=0, keepdims=True))
            return worst

        worst = lax.fori_loop(0, nb // 4, one, jnp.zeros((1, block), F32))
        return count + 1, jnp.sum(worst)

    def unsettled(state):
        count, err = state
        return (count < 30) & jnp.logical_not(err < 1e-6)

    _, err = lax.while_loop(unsettled, settle, (jnp.int32(0), jnp.float32(1.0)))

    @pl.when(jnp.logical_not(err < 1e-6))
    def _():
        invert_direct(s_ref, x_ref, block)

    def finish(b, _):
        hi, lo = split(x_ref[b] * d_ref[b])
        sh_ref[b] = hi
        sl_ref[b] = lo
        return 0

    lax.fori_loop(0, nb, finish, 0)


def solve_kernel(step, *refs):
    if step:
        (g_ref, order_ref, gp_ref, dp_ref, out_ref,
         k_ref, s_ref, sh_ref, sl_ref, x_ref, d_ref, start_ref) = refs
    else:
        (g_ref, out_ref,
         k_ref, s_ref, sh_ref, sl_ref, x_ref, d_ref, start_ref) = refs
    width, outs = out_ref.shape
    nb, block = s_ref.shape[:2]
    depth = g_ref.shape[1] - 2 * outs
    scale = 0.25 / math.sqrt(depth)
    chunk = 2 * block
    feat = slice(2 * outs, 2 * outs + depth)
    start_ref[...] = g_ref[:, :outs].astype(F32) + g_ref[:, outs : 2 * outs].astype(F32)
    eye = lax.broadcasted_iota(jnp.int32, (block, block), 0) == lax.broadcasted_iota(
        jnp.int32, (block, block), 1
    )

    def rows(ref, i, size):
        return ref[pl.ds(pl.multiple_of(i * size, size), size), feat]

    if step:
        def earlier(i, _):
            def part(j, acc):
                tile = kernel_of(rows(g_ref, i, chunk), rows(gp_ref, j, chunk), scale)
                at = pl.multiple_of(j * chunk, chunk)
                return acc + dot(tile.astype(BF), dp_ref[pl.ds(at, chunk), :])

            acc = lax.fori_loop(0, width // chunk, part, jnp.zeros((chunk, outs), F32))
            at = pl.ds(pl.multiple_of(i * chunk, chunk), chunk)
            start_ref[at, :] = start_ref[at, :] - acc
            return 0

        lax.fori_loop(0, width // chunk, earlier, 0)

        def again(n, _):
            i, j = n // nb, n % nb

            @pl.when(order_ref[1, i] == order_ref[0, j])
            def _():
                at = pl.ds(pl.multiple_of(i * block, block), block)
                old = dp_ref[pl.ds(pl.multiple_of(j * block, block), block), :]
                start_ref[at, :] = start_ref[at, :] - ridge * old.astype(F32)

            return 0

        lax.fori_loop(0, nb * nb, again, 0)

    def diagonal(i, _):
        x = rows(g_ref, i, block)
        s_ref[i] = kernel_of(x, x, scale) + jnp.where(eye, ridge, 0.0)
        return 0

    lax.fori_loop(0, nb, diagonal, 0)

    def lower(i, _):
        def part(j, _):
            tile = kernel_of(rows(g_ref, i, chunk), rows(g_ref, j, chunk), scale).astype(BF)
            k_ref[
                pl.ds(pl.multiple_of(i * chunk, chunk), chunk),
                pl.ds(pl.multiple_of(j * chunk, chunk), chunk),
            ] = tile
            return 0

        lax.fori_loop(0, i + 1, part, 0)
        return 0

    lax.fori_loop(0, width // chunk, lower, 0)
    invert_all(s_ref, sh_ref, sl_ref, x_ref, d_ref, block)
    done = None
    for j in range(nb):
        at = slice(j * block, (j + 1) * block)
        rest = start_ref[at, :]
        if done is not None:
            rest = rest - done
        if j:
            last = slice((j - 1) * block, j * block)
            rest = rest - dot(k_ref[at, last], out_ref[last, :])
        hi, lo = split(rest)
        new = dot(sh_ref[j], lo) + dot(sl_ref[j], hi) + dot(sh_ref[j], hi)
        if 0 < j < nb - 1:
            done = dot(k_ref[(j + 1) * block : (j + 2) * block, : j * block], out_ref[: j * block, :])
        out_ref[at, :] = new.astype(BF)


def solve(step, outs, block, g, *earlier):
    width = g.shape[0]
    nb = width // block
    specs = [VMEM, SMEM, VMEM, VMEM] if step else [VMEM]
    return pl.pallas_call(
        functools.partial(solve_kernel, step),
        out_shape=jax.ShapeDtypeStruct((width, outs), BF),
        in_specs=specs,
        out_specs=VMEM,
        scratch_shapes=[
            pltpu.VMEM((width, width), BF),
            pltpu.VMEM((nb, block, block), F32),
            pltpu.VMEM((nb, block, block), BF),
            pltpu.VMEM((nb, block, block), BF),
            pltpu.VMEM((nb, block, block), F32),
            pltpu.VMEM((nb, block, block), F32),
            pltpu.VMEM((width, outs), F32),
        ],
    )(g, *earlier)


def project_kernel(base_ref, ids_ref, x_ref, p_ref, a_ref, g0_ref, g1_ref, d0_ref, d1_ref,
                   np_ref, na_ref, xt_ref):
    outs, frames = p_ref.shape
    depth = x_ref.shape[0]
    block = ids_ref.shape[1]
    width = d0_ref.shape[0]
    scale = 0.25 / math.sqrt(depth)
    feat = slice(2 * outs, 2 * outs + depth)
    xt_ref[...] = x_ref[...].astype(F32).T.astype(BF)
    sub = lax.broadcasted_iota(jnp.int32, (frames, block), 0) + base_ref[0]
    nb = width // block
    both = (jnp.zeros((frames, outs), F32), jnp.zeros((frames, outs), F32))
    for step, (g_ref, d_ref) in enumerate(((g0_ref, d0_ref), (g1_ref, d1_ref))):
        def part(j, acc):
            pred, coef = acc
            at = pl.ds(pl.multiple_of(j * block, block), block)
            new = d_ref[at, :]
            tile = kernel_of(xt_ref[...], g_ref[at, feat], scale).astype(BF)
            hot = jnp.where(ids_ref[pl.ds(step * nb + j, 1), :] == sub, 1.0, 0.0).astype(BF)
            return pred + dot(tile, new), coef + dot(hot, new)

        both = lax.fori_loop(0, nb, part, both)
    np_ref[...] = p_ref[...] + both[0].T
    na_ref[...] = a_ref[...] + both[1].T


def project(base, ids, features, predictions, coeffs, g0, g1, d0, d1):
    shape = jax.ShapeDtypeStruct(predictions.shape, F32)
    return pl.pallas_call(
        project_kernel,
        out_shape=(shape, shape),
        in_specs=[SMEM] + [VMEM] * 8,
        out_specs=(VMEM, VMEM),
        scratch_shapes=[pltpu.VMEM((features.shape[1], features.shape[0]), BF)],
    )(base, ids, features, predictions, coeffs, g0, g1, d0, d1)


def per_device(features, targets, predictions, coeffs, members, order):
    frames = features.shape[1]
    outs = targets.shape[0]
    block = members.shape[1]
    base = (lax.axis_index(ALL) * frames).astype(jnp.int32).reshape(1)
    ids = members[order.reshape(-1)].astype(jnp.int32)
    nb = order.shape[1]
    g = []
    for step in range(STEPS):
        mine = pick(base, ids[step * nb : (step + 1) * nb], features, targets, predictions, coeffs)
        if g:
            g[0], mine = lax.optimization_barrier((g[0], mine))
        g.append(lax.psum(mine, ALL))
    d0 = solve(0, outs, block, g[0])
    d1 = solve(1, outs, block, g[1], order.astype(jnp.int32), g[0], d0)
    return project(base, ids, features, predictions, coeffs, g[0], g[1], d0, d1)


def solution(mesh):
    torus = Mesh(mesh.devices.reshape(8, 2, mesh.shape["row"]), ("ctr_0", "ctr_1", "row"))
    return jax.shard_map(
        per_device,
        mesh=torus,
        in_specs=(P(None, ALL), P(None, ALL), P(None, ALL), P(None, ALL), P(), P()),
        out_specs=(P(None, ALL), P(None, ALL)),
        check_vma=False,
    )
```

time: 828 us -> 660 us (0.80)
  starting transfers between devices: 206 us -> 0.08 us
  Pallas kernels: 0 us -> 148 us
  waiting for transfers between devices: 353 us -> 495 us
  other arithmetic: 94.7 us -> 0.01 us
  local copies, waits for them, and re-layouts: 79.8 us -> 2.17 us
  blocking collectives: 49 us -> 0 us
  matrix products: 26.6 us -> 0 us
    psum x0 -> x2, waiting for transfers between devices: none -> 495 us  [per_device(): g.append(lax.psum(mine, ALL))]
    ppermute x30 -> x0, waiting for transfers between devices: 183 us -> none  [from_behind(): return lax.ppermute(array, axis, pairs)]
    pallas_call x0 -> x5, Pallas kernels: none -> 148 us  [the longest x2 115 us: solve(): pl.pallas_call(functools.partial(solve_kernel, step), out_shape=jax.Shape...]
    all_to_all x6 -> x0, waiting for transfers between devices: 136 us -> none  [the longest x4 105 us: sent_to_all(): lax.all_to_all(jnp.broadcast_to(array[None], (size, *array.shape)), axis,...]
    ppermute x30 -> x0, starting transfers between devices: 127 us -> none  [from_behind(): return lax.ppermute(array, axis, pairs)]
    all_to_all x6 -> x0, starting transfers between devices: 79.4 us -> none  [the longest x4 65.9 us: sent_to_all(): lax.all_to_all(jnp.broadcast_to(array[None], (size, *array.shape)), axis,...]
    gather x10 -> x1, local copies, waits for them, and re-layouts: 63.1 us -> 0.57 us  [per_device(): ids = members[order.reshape(-1)].astype(jnp.int32)]
    all_to_all x4 -> x0, blocking collectives: 49 us -> none  [the longest x2 26.9 us: sum_at_owner(): pieces = lax.all_to_all(split_up(array, dim, size), axis, 0, 0, tiled=True)]
  transfers between devices with their start and end apart: 40 -> 2, of which waited for: 39 -> 2; matrix products, arithmetic and copies ran while one was open for 15% -> 0% of each run, Pallas kernels for 0% -> 7%
where the time goes in v1:
time: 660 us; the launch traced here: 659 us
  waiting for transfers between devices  495 us (75%)
  Pallas kernels  148 us (22%)
  between operations  14.1 us (2%)
    psum x2, waiting for transfers between devices, per_device(): g.append(lax.psum(mine, ALL))  495 us
    pallas_call x2, Pallas kernels, solve(): pl.pallas_call(functools.partial(solve_kernel, step), out_shape=jax.Shape...  115 us
    pallas_call x1, Pallas kernels, project(): pl.pallas_call(project_kernel, out_shape=(shape, shape), in_specs=[SMEM]...  22.8 us
  transfers between devices with their start and end apart: 2, of which 2 were waited for; matrix products, arithmetic and copies ran while one was open for 0% of the time, Pallas kernels for 7%

profile of v1, /device:TPU:1, one launch (start us, length us, event | category | flops | bytes accessed | tf_op | source)
XLA Modules:
  0.0 659.3 jit_solution(1618165552282742069)
XLA Ops:
  7.2 0.0 copy-start
  7.2 0.0 all-reduce.3.cloned.1.call-start
  7.2 0.8 reshape.39
  8.1 0.2 copy-done
  8.2 0.6 gather_fusion
  8.8 0.0 copy-start.1
  8.8 0.6 fusion.1
  9.4 5.1 shard_map.77
  14.5 0.0 all-reduce.3.cloned.1.call-update
  14.5 0.0 copy-done.1
  14.5 0.0 all-reduce.5.cloned.1.call-start
  14.6 5.1 shard_map.78
  19.7 263.4 %all-reduce.3.cloned.1.call-done.refs_0_.refs_2_.g0_ref = bf16[2048,696]{1,0:T(8,128)(2,1)} async-done(((bf16[2048,696]{1,0:T(8,128)(2,1)}), bf16[2048,696]{1,0:T(8,128)(2,1)}) %all-reduce.3.cloned.1.call-update) | async-done | bytes 2850832 | tf_op jit(solution)/shard_map/psum | solution.py:296
  283.1 0.0 all-reduce.5.cloned.1.call-update
  283.2 38.9 %shard_map.79.refs_3_.d0_ref = bf16[2048,128]{1,0:T(8,128)(2,1)} custom-call(bf16[2048,696]{1,0:T(8,128)(2,1)} %all-reduce.3.cloned.1.call-done.refs_0_.refs_2_.g0_ref), custom_call_target="tpu_custom_call" | custom-call | tf_op jit(solution)/shard_map/pallas_call | solution.py:230
  322.1 231.8 %all-reduce.5.cloned.1.call-done.refs_0_.g1_ref = bf16[2048,696]{1,0:T(8,128)(2,1)} async-done(((bf16[2048,696]{1,0:T(8,128)(2,1)}), bf16[2048,696]{1,0:T(8,128)(2,1)}) %all-reduce.5.cloned.1.call-update) | async-done | bytes 2850832 | tf_op jit(solution)/shard_map/psum | solution.py:296
  553.9 75.8 %shard_map.80.d1_ref = bf16[2048,128]{1,0:T(8,128)(2,1)} custom-call(bf16[2048,696]{1,0:T(8,128)(2,1)} %all-reduce.5.cloned.1.call-done.refs_0_.g1_ref, s32[2,16]{1,0:T(2,128)} %refs_1_.1, bf16[2048,696]{1,0:T(8,128)(2,1)} %all-reduce.3.cloned.1.call-done.refs_0_.refs_2_.g0_ref, bf16[2048,128]{1,0:T(8,128)(2,1)} %shard_map.79.refs_3_.d0_ref), custom_call_target="tpu_custom_call" | custom-call | tf_op jit(solution)/shard_map/pallas_call | solution.py:230
  629.7 22.8 %shard_map.81 = (f32[128,512]{1,0:T(8,128)}, f32[128,512]{1,0:T(8,128)}) custom-call(s32[1]{0:T(128)} %bitcast.base_ref, s32[32,128]{1,0:T(8,128)} %copy-done.1, bf16[440,512]{1,0:T(8,128)(2,1)} %x_ref.5, f32[128,512]{1,0:T(8,128)} %p_ref.5, f32[128,512]{1,0:T(8,128)} %a_ref.5, bf16[2048,696]{1,0:T(8,128)(2,1)} %all-reduce.3.cloned.1.call-done.refs_0_.refs_2_.g0_ref, ...), custom_call_target="tpu_custom_call" | custom-call | tf_op jit(solution)/shard_map/pallas_call | solution.py:275
  (2 shorter events, 0.0 us)
Async XLA Ops:
  7.2 1.1 copy-start
  7.2 276.0 %all-reduce.3.cloned.1.call-start = ((), (), s32[]{:S(2)}) async-start(), calls=%async_computation | async-start | bytes 6291456 | tf_op jit(solution)/shard_map/psum | solution.py:296
  8.8 5.7 copy-start.1
  14.5 539.4 %all-reduce.5.cloned.1.call-start = ((), (), s32[]{:S(2)}) async-start(), calls=%async_computation.1 | async-start | bytes 6291456 | tf_op jit(solution)/shard_map/psum | solution.py:296
Sparse Core Ops, SparseCore 0:
  14.7 268.4 all-reduce.2
  288.6 265.2 all-reduce.4
